TPU v7x, 128 devices: a whole 4x4x4 slice. The times are simulated.
128 devices in a mesh: dp: 16 (over x_lo, y, core), shard: 8 (over x_hi, z).
Axes of the slice: x: 4 (x_hi: 2, x_lo: 2; x = x_hi * 2 + x_lo), y: 4, z: 4, core: 2. Of those that a mesh axis runs over, the one named last changes fastest.
Arguments:
- grad_parts: bfloat16 [16, 16, 1024, 1024], P('dp', None, 'shard'), may hold values from -6 to 6
- first_moment: float32 [16384, 1024], P(('dp', 'shard')), may hold values from -6 to 6
- second_moment: float32 [16384, 1024], P(('dp', 'shard')), may hold values from 0.1 to 16
- master: float32 [16384, 1024], P(('dp', 'shard')), may hold values from -6 to 6
- old_map: int32 [16384], replicated, may hold values from 0 to 16383, as said below
- new_map: int32 [16384], replicated, may hold values from 0 to 16383, as said below
Outputs:
- new_first: float32 [16384, 1024], P(('dp', 'shard'))
- new_second: float32 [16384, 1024], P(('dp', 'shard'))
- new_master: float32 [16384, 1024], P(('dp', 'shard'))
- weights_half: bfloat16 [16384, 1024], P('dp')
Inputs may be any that keep to these rules, and one draw needn't show every extreme that they name: old_map is a permutation of the 16384 block numbers. Row r of either layout belongs to device r // 128. Of the blocks that one device holds in the old layout, exactly one belongs to each device in the new layout. new_map is a permutation of the 16384 block numbers, with the property stated for old_map.
All inputs are finite; a program needn't handle non-finite values.
Results may differ from a plain program's by a relative error of at most 0.0085.
Values may be sent and summed in bfloat16 or wider, within the bound.
A program may use at most 64 MiB of HBM per device.

v0:
```python
import jax
import jax.numpy as jnp
from jax import lax
from jax.sharding import PartitionSpec as P

beta_one = 0.9
beta_two = 0.95
learning_rate = 0.05
decay_rate = 0.1
epsilon = 1e-08
step_count = 4


def adamw(moment_one, moment_two, weights, gradient):
    new_one = beta_one * moment_one + (1.0 - beta_one) * gradient
    new_two = beta_two * moment_two + (1.0 - beta_two) * gradient * gradient
    unbiased_one = new_one / (1.0 - beta_one**step_count)
    unbiased_two = new_two / (1.0 - beta_two**step_count)
    updated = weights - learning_rate * (
        unbiased_one / (jnp.sqrt(unbiased_two) + epsilon) + decay_rate * weights
    )
    return (new_one, new_two, updated)


def owner_table(blocks, mapping, device_count, span):
    grid = mapping.reshape(device_count, span)
    found = jnp.any(blocks[:, None, None] == grid[None, :, :], axis=2)
    return found.astype(jnp.float32)


def local(grad_parts, first_moment, second_moment, master, old_map, new_map):
    groups = lax.axis_size("dp")
    shard_width = lax.axis_size("shard")
    device_count = groups * shard_width
    my_index = lax.axis_index("dp") * shard_width + lax.axis_index("shard")
    span = first_moment.shape[0]
    block_len = first_moment.shape[1]
    summed_grad = lax.psum_scatter(
        grad_parts[0].astype(jnp.float32).astype(jnp.bfloat16),
        "dp",
        scatter_dimension=0,
        tiled=True,
    ).astype(jnp.float32)[0]
    local_blocks = lax.dynamic_slice_in_dim(old_map, my_index * span, span)
    route = owner_table(local_blocks, new_map, device_count, span)
    packed = jnp.stack([first_moment, second_moment, master], axis=1).reshape(span, 3 * block_len)
    outgoing = jnp.dot(
        route.T, packed, precision=lax.Precision.HIGHEST, preferred_element_type=jnp.float32
    )
    outgoing = outgoing.reshape(device_count, 3, block_len)
    incoming = lax.all_to_all(outgoing, ("dp", "shard"), split_axis=0, concat_axis=0, tiled=True)
    incoming = incoming.reshape(device_count, 3 * block_len)
    wanted = lax.dynamic_slice_in_dim(new_map, my_index * span, span)
    pick = owner_table(wanted, old_map, device_count, span)
    states = jnp.dot(
        pick, incoming, precision=lax.Precision.HIGHEST, preferred_element_type=jnp.float32
    )
    states = states.reshape(span, 3, block_len)
    new_one, new_two, updated = adamw(states[:, 0], states[:, 1], states[:, 2], summed_grad)
    gathered = lax.all_gather(updated.astype(jnp.bfloat16), "shard", axis=0, tiled=True)
    return (new_one, new_two, updated, gathered)


def solution(mesh):
    placed = (
        P("dp", None, "shard", None),
        P(("dp", "shard"), None),
        P(("dp", "shard"), None),
        P(("dp", "shard"), None),
        P(),
        P(),
    )
    return jax.shard_map(
        local,
        mesh=mesh,
        in_specs=placed,
        out_specs=(
            P(("dp", "shard"), None),
            P(("dp", "shard"), None),
            P(("dp", "shard"), None),
            P("dp", None),
        ),
        check_vma=False,
    )
```

profile of v0, /device:TPU:1, one launch (start us, length us, event | category | flops | bytes accessed | tf_op | source)
XLA Modules:
  0.0 161.5 jit_solution(11646434920903755506)
XLA Ops:
  7.2 0.0 reduce-scatter.2.cloned.1.call-start
  7.2 0.0 copy-start
  7.2 0.0 copy-start.1
  7.2 0.7 reduce-scatter.2.cloned.1.call-update
  7.9 0.0 copy-start.2
  7.9 0.3 copy-done
  8.3 0.0 copy-start.4
  8.3 0.0 copy-start.3
  8.3 0.2 copy.19
  8.5 0.0 copy-done.1
  8.5 0.2 copy.20
  8.7 0.4 copy-done.2
  9.0 0.2 copy.21
  9.2 0.0 copy-done.4
  9.2 0.1 dynamic_slice.7
  9.3 0.0 copy-done.3
  9.3 2.4 %compare_reduce_fusion = pred[128,128]{1,0:T(8,128)(4,1)S(1)} fusion(s32[128,128]{1,0:T(8,128)S(1)} %bitcast.54, s32[128]{0:T(128)S(1)} %dynamic_slice.7), kind=kLoop, calls=%fused_computation | loop fusion | flops 4177920 | bytes 82432 | tf_op jit(solution)/shard_map/reduce_or | solution.py:27
  11.7 1.0 fusion
  12.7 2.4 %copy.23 = f32[128,3,1024]{2,1,0:T(4,128)} copy(f32[128,3,1024]{2,0,1:T(8,128)S(1)} %fusion) | data formatting | bytes 3145728 | tf_op jit(solution)/shard_map/dot_general | solution.py:47
  15.1 11.5 %all-to-all-start = ((f32[128,3,1024]{2,1,0:T(4,128)}), f32[128,3,1024]{2,1,0:T(4,128)S(1)}, u32[]{:S(2)}, u32[]{:S(2)}) async-start(f32[128,3,1024]{2,1,0:T(4,128)} %copy.23), calls=%async_computation | async-start | bytes 4194304 | tf_op jit(solution)/shard_map/all_to_all | solution.py:51
  26.6 0.0 all-gather.2.cloned.1.call-start
  26.6 0.1 dynamic_slice.6
  26.7 2.4 %compare_reduce_fusion.1 = pred[128,128]{1,0:T(8,128)(4,1)S(1)} fusion(s32[128,128]{1,0:T(8,128)S(1)} %bitcast.55, s32[128]{0:T(128)S(1)} %dynamic_slice.6), kind=kLoop, calls=%fused_computation.1 | loop fusion | flops 4177920 | bytes 82432 | tf_op jit(solution)/shard_map/reduce_or | solution.py:27
  29.1 30.2 %all-to-all-done = f32[128,3,1024]{2,1,0:T(4,128)S(1)} async-done(((f32[128,3,1024]{2,1,0:T(4,128)}), f32[128,3,1024]{2,1,0:T(4,128)S(1)}, u32[]{:S(2)}, u32[]{:S(2)}) %all-to-all-start) | async-done | bytes 1572896 | tf_op jit(solution)/shard_map/all_to_all | solution.py:51
  59.3 1.6 %copy.24 = f32[128,3,1024]{0,2,1:T(8,128)} copy(f32[128,3,1024]{2,1,0:T(4,128)S(1)} %all-to-all-done) | data formatting | bytes 3145728 | tf_op jit(solution)/shard_map/all_to_all | solution.py:51
  61.0 2.4 %fusion.5 = f32[128,3,1024]{2,0,1:T(8,128)S(1)} fusion(f32[128,3,1024]{0,2,1:T(8,128)} %copy.24, pred[128,128]{1,0:T(8,128)(4,1)S(1)} %compare_reduce_fusion.1), kind=kOutput, calls=%fused_computation.8 | convolution fusion | flops 603979776 | bytes 3162112 | tf_op jit(solution)/shard_map/dot_general | solution.py:55
  63.3 29.1 %reduce-scatter.2.cloned.1.call-done = bf16[1,128,1024]{2,1,0:T(8,128)(2,1)} async-done(((bf16[16,128,1024]{2,1,0:T(8,128)(2,1)}), bf16[1,128,1024]{2,1,0:T(8,128)(2,1)}) %reduce-scatter.2.cloned.1.call-update) | async-done | bytes 262160 | tf_op jit(solution)/shard_map/reduce_scatter | solution.py:38
  92.4 2.4 %fusion.14 = (bf16[128,1024]{1,0:T(8,128)(2,1)}, f32[128,1024]{1,0:T(8,128)}, f32[128,1024]{1,0:T(8,128)}, f32[128,1024]{1,0:T(8,128)}) fusion(f32[128,3,1024]{2,0,1:T(8,128)S(1)} %fusion.5, bf16[1,128,1024]{2,1,0:T(8,128)(2,1)} %reduce-scatter.2.cloned.1.call-done), kind=kLoop, calls=%fused_computation.24 | loop fusion | flops 2228224 | bytes 3670016 | tf_op jit(solution)/shard_map/convert_element_type | solution.py:60
  94.8 0.0 all-gather.2.cloned.1.call-update
  94.8 56.8 %all-gather.2.cloned.1.call-done = bf16[1024,1024]{1,0:T(8,128)(2,1)} async-done(((bf16[128,1024]{1,0:T(8,128)(2,1)}), bf16[1024,1024]{1,0:T(8,128)(2,1)}) %all-gather.2.cloned.1.call-update) | async-done | bytes 2097168 | tf_op jit(solution)/shard_map/all_gather | solution.py:60
  151.6 3.1 %copy.28 = bf16[1024,1024]{1,0:T(8,128)(2,1)} copy(bf16[1024,1024]{1,0:T(8,128)(2,1)} %all-gather.2.cloned.1.call-done) | data formatting | bytes 4194304
Async XLA Ops:
  7.2 85.2 %reduce-scatter.2.cloned.1.call-start = ((), (), s32[]{:S(2)}) async-start(), calls=%async_computation.2 | async-start | bytes 4456448 | tf_op jit(solution)/shard_map/reduce_scatter | solution.py:38
  7.2 1.0 copy-start
  7.2 1.2 copy-start.1
  7.9 1.1 copy-start.2
  8.3 1.0 copy-start.4
  8.3 1.1 copy-start.3
  15.1 44.3 %all-to-all-start = ((f32[128,3,1024]{2,1,0:T(4,128)}), f32[128,3,1024]{2,1,0:T(4,128)S(1)}, u32[]{:S(2)}, u32[]{:S(2)}) async-start(f32[128,3,1024]{2,1,0:T(4,128)} %copy.23), calls=%async_computation | async-start | bytes 4194304 | tf_op jit(solution)/shard_map/all_to_all | solution.py:51
  26.6 125.0 %all-gather.2.cloned.1.call-start = ((), (), s32[]{:S(2)}) async-start(), calls=%async_computation.3 | async-start | bytes 2359296 | tf_op jit(solution)/shard_map/all_gather | solution.py:60
Sparse Core Ops, SparseCore 0:
  10.4 81.9 reduce-scatter.1
  95.3 56.2 all-gather.1
where the time goes:
time: 162 us
  waiting for transfers between devices  117 us (72%)
  between operations  14.1 us (9%)
  starting transfers between devices  11.6 us (7%)
  local copies, waits for them, and re-layouts  8.54 us (5%)
  other arithmetic  7.22 us (4%)
  matrix products  3.3 us (2%)
    all_gather x1, waiting for transfers between devices, local(): lax.all_gather(updated.astype(jnp.bfloat16), 'shard', axis=0, tiled=True)  56.8 us
    all_to_all x1, waiting for transfers between devices, local(): lax.all_to_all(outgoing, ('dp', 'shard'), split_axis=0, concat_axis=0, ti...  30.2 us
    reduce_scatter x1, waiting for transfers between devices, local(): lax.psum_scatter(grad_parts[0].astype(jnp.float32).astype(jnp.bfloat16),...  29.1 us
    all_to_all x1, starting transfers between devices, local(): lax.all_to_all(outgoing, ('dp', 'shard'), split_axis=0, concat_axis=0, ti...  11.5 us
    reduce_or x2, other arithmetic, owner_table(): found = jnp.any(blocks[:, None, None] == grid[None, :, :], axis=2)  4.78 us
    unnamed x14, local copies, waits for them, and re-layouts  4.36 us
  transfers between devices with their start and end apart: 3, of which 3 were waited for; matrix products, arithmetic and copies ran while one was open for 8% of the time, Pallas kernels for 0%

commit v1 on v0

v1 whole, which is shorter than its diff:
```python
import functools

import jax
import jax.numpy as jnp
from jax import lax
from jax.experimental import pallas as pl
from jax.experimental.pallas import tpu as pltpu
from jax.sharding import PartitionSpec as P

beta_one = 0.9
beta_two = 0.95
learning_rate = 0.05
decay_rate = 0.1
epsilon = 1e-08
step_count = 4

MESH = pl.DeviceIdType.MESH
BPD = 128
BLK = 1024
f32 = jnp.float32
bf16 = jnp.bfloat16

CHUNKS = ((0, 32, "y", "x"), (32, 32, "x", "z"), (64, 32, "y", "x"), (96, 32, "x", "z"))


def adamw(moment_one, moment_two, weights, gradient):
    new_one = beta_one * moment_one + (1.0 - beta_one) * gradient
    new_two = beta_two * moment_two + (1.0 - beta_two) * gradient * gradient
    unbiased_one = new_one / (1.0 - beta_one**step_count)
    unbiased_two = new_two / (1.0 - beta_two**step_count)
    updated = weights - learning_rate * (
        unbiased_one / (jnp.sqrt(unbiased_two) + epsilon) + decay_rate * weights
    )
    return (new_one, new_two, updated)


def owners(wanted_row, table_ref, turned_ref):
    wanted = jnp.broadcast_to(wanted_row, (BPD, BPD)).T
    turned_ref[...] = table_ref[...].T

    def step(k, found):
        return jnp.where(wanted == turned_ref[pl.ds(k, 1), :], 1.0, found)

    return lax.fori_loop(0, BPD, step, jnp.zeros((BPD, BPD), f32), unroll=8)


def swap_matrix():
    row = lax.broadcasted_iota(jnp.int32, (BPD, BPD), 0)
    col = lax.broadcasted_iota(jnp.int32, (BPD, BPD), 1)
    turned = (row & 64) | ((row & 7) << 3) | ((row >> 3) & 7)
    return jnp.where(turned == col, 1.0, 0.0).astype(bf16)


def kernel(
    grad, first, second, master, old_map, new_map,
    out_one, out_two, out_master, out_half,
    states, old_ref, new_ref, turned, own, other, pair, from_y, from_x, part, kept,
    send_a, recv_a, send_b, recv_b,
    load_sem, core_s, core_r, sum_s, sum_r, a_s, a_r, b_s, b_r, gat_s, gat_r, fwd_s, fwd_r,
):
    dp = lax.axis_index("dp")
    sh = lax.axis_index("shard")
    xl, yc = dp // 8, dp % 8
    y, c = yc // 2, yc % 2
    xh, z = sh // 4, sh % 4
    me = dp * 8 + sh

    def at_y(k):
        return (xl * 8 + lax.rem(y + k, 4) * 2 + c, sh)

    def at_z(k):
        return (dp, xh * 4 + lax.rem(z + k, 4))

    x_near = ((1 - xl) * 8 + yc, sh)
    x_far = (dp, (1 - xh) * 4 + z)
    core_mate = (xl * 8 + y * 2 + (1 - c), sh)
    a_peers = [(xl * 8 + lax.rem(yc + k, 8), sh) for k in range(1, 8)]
    place = xl * 8 + sh
    b_places = [lax.rem(place + k, 16) for k in range(1, 16)]
    b_peers = [((p // 8) * 8 + yc, p % 8) for p in b_places]

    barrier = pltpu.get_barrier_semaphore()
    for peer in a_peers + b_peers:
        pl.semaphore_signal(barrier, inc=1, device_id=peer, device_id_type=MESH)

    loads = [
        pltpu.make_async_copy(new_map, new_ref, load_sem.at[0]),
        pltpu.make_async_copy(old_map, old_ref, load_sem.at[1]),
        pltpu.make_async_copy(first, states.at[0], load_sem.at[2]),
        pltpu.make_async_copy(second, states.at[1], load_sem.at[3]),
        pltpu.make_async_copy(master, states.at[2], load_sem.at[4]),
        pltpu.make_async_copy(grad.at[:, c], own, load_sem.at[5]),
    ]
    for load in loads:
        load.start()
    loads[0].wait()
    loads[1].wait()
    route = owners(old_ref[pl.ds(me, 1), :], new_ref, turned).T.astype(bf16)

    pl.semaphore_wait(barrier, 22)

    def remote(src, dst, s_sem, r_sem, peer):
        copy = pltpu.make_async_remote_copy(
            src_ref=src, dst_ref=dst, send_sem=s_sem, recv_sem=r_sem,
            device_id=peer, device_id_type=MESH,
        )
        copy.start()
        return copy

    sent = []

    core = []
    for i, (r0, n, _, _) in enumerate(CHUNKS):
        rows = pl.ds(r0, n)
        core.append(
            remote(grad.at[:, 1 - c, rows], other.at[:, rows], core_s.at[i], core_r.at[i], core_mate)
        )
    sent += core

    for j in range(3):
        loads[2 + j].wait()
        moved = jnp.dot(route, states[j].astype(bf16), preferred_element_type=f32)
        send_a[:, :, :, j * BLK : (j + 1) * BLK] = moved.reshape(2, 8, 8, BLK).astype(bf16)
    stage_a = []
    for k in range(1, 8):
        to = lax.rem(yc + k, 8)
        stage_a.append(
            remote(send_a.at[:, to], recv_a.at[:, yc], a_s.at[k - 1], a_r.at[k - 1], a_peers[k - 1])
        )
    sent += stage_a
    keep_a = pltpu.make_async_copy(send_a.at[:, yc], recv_a.at[:, yc], load_sem.at[0])
    keep_a.start()

    loads[5].wait()
    steps_one = []
    for i, (r0, n, order, _) in enumerate(CHUNKS):
        rows = pl.ds(r0, n)
        core[i].wait_recv()

        def add_pair(q, carry, rows=rows):
            pair[q, rows, :] = own[q, rows, :] + other[q, rows, :]
            return carry

        lax.fori_loop(0, 8, add_pair, 0)
        if order == "x":
            copies = [
                remote(
                    pair.at[pl.ds((1 - xl) * 4, 4), rows], from_x.at[:, rows],
                    sum_s.at[i, 0], sum_r.at[i, 0], x_near,
                )
            ]
        else:
            copies = []
            for k in range(1, 4):
                to = lax.rem(y + k, 4)
                for side in range(2):
                    copies.append(
                        remote(
                            pair.at[side * 4 + to, rows], from_y.at[k - 1, side, rows],
                            sum_s.at[i, (k - 1) * 2 + side], sum_r.at[i, (k - 1) * 2 + side], at_y(k),
                        )
                    )
        steps_one.append(copies)
        sent += copies

    swap = swap_matrix()
    for copy in stage_a:
        copy.wait_recv()
    keep_a.wait()
    for j in range(3):
        cols = slice(j * BLK, (j + 1) * BLK)
        came = recv_a[:, :, :, cols].astype(f32).reshape(BPD, BLK).astype(bf16)
        moved = jnp.dot(swap, came, preferred_element_type=f32)
        send_b[:, :, cols] = moved.reshape(16, 8, BLK).astype(bf16)
    stage_b = []
    for k in range(1, 16):
        stage_b.append(
            remote(send_b.at[b_places[k - 1]], recv_b.at[place], b_s.at[k - 1], b_r.at[k - 1], b_peers[k - 1])
        )
    sent += stage_b
    keep_b = pltpu.make_async_copy(send_b.at[place], recv_b.at[place], load_sem.at[1])
    keep_b.start()

    steps_two = []
    for i, (r0, n, order, _) in enumerate(CHUNKS):
        rows = pl.ds(r0, n)
        for copy in steps_one[i]:
            copy.wait_recv()
        copies = []
        if order == "x":
            for k in range(1, 4):
                to = lax.rem(y + k, 4)
                part[k - 1, rows, :] = pair[xl * 4 + to, rows, :] + from_x[to, rows, :]
                copies.append(
                    remote(
                        part.at[k - 1, rows], from_y.at[k - 1, 0, rows],
                        sum_s.at[i, k], sum_r.at[i, k], at_y(k),
                    )
                )
            kept[rows, :] = pair[xl * 4 + y, rows, :].astype(f32) + from_x[y, rows, :].astype(f32)
        else:
            def total(side, rows=rows):
                value = pair[side * 4 + y, rows, :].astype(f32)
                for k in range(3):
                    value = value + from_y[k, side, rows, :].astype(f32)
                return value

            part[0, rows, :] = total(1 - xl).astype(bf16)
            copies.append(
                remote(part.at[0, rows], from_x.at[0, rows], sum_s.at[i, 6], sum_r.at[i, 6], x_near)
            )
            kept[rows, :] = total(xl)
        steps_two.append(copies)
        sent += copies

    pick = owners(new_ref[pl.ds(me, 1), :], old_ref, turned).astype(bf16)
    pick = jnp.dot(pick, swap, preferred_element_type=f32).astype(bf16)
    for copy in stage_b:
        copy.wait_recv()
    keep_b.wait()
    for j in range(3):
        cols = slice(j * BLK, (j + 1) * BLK)
        came = recv_b[:, :, cols].astype(f32).reshape(BPD, BLK).astype(bf16)
        states[j] = jnp.dot(pick, came, preferred_element_type=f32)

    gathers = []
    for i, (r0, n, order, _) in enumerate(CHUNKS):
        rows = pl.ds(r0, n)
        for copy in steps_two[i]:
            copy.wait_recv()
        summed = kept[rows, :]
        if order == "x":
            for k in range(3):
                summed = summed + from_y[k, 0, rows, :].astype(f32)
        else:
            summed = summed + from_x[0, rows, :].astype(f32)
        new_one, new_two, updated = adamw(
            states[0, rows, :], states[1, rows, :], states[2, rows, :], summed
        )
        out_half[sh, rows, :] = updated.astype(bf16)
        block = out_half.at[sh, rows]
        copies = [remote(block, block, gat_s.at[i, 0], gat_r.at[i, 0], x_far)]
        for k in range(1, 4):
            copies.append(remote(block, block, gat_s.at[i, k], gat_r.at[i, k], at_z(k)))
        gathers.append(copies)
        sent += copies
        out_one[rows, :] = new_one
        out_two[rows, :] = new_two
        out_master[rows, :] = updated

    forwards = []
    for i, (r0, n, _, order) in enumerate(CHUNKS):
        rows = pl.ds(r0, n)
        copies = []
        if order == "x":
            gathers[i][0].wait_recv()
            block = out_half.at[(1 - xh) * 4 + z, rows]
            for k in range(1, 4):
                copies.append(remote(block, block, fwd_s.at[i, k - 1], fwd_r.at[i, k - 1], at_z(k)))
        for k in range(1, 4):
            gathers[i][k].wait_recv()
            if order == "z":
                block = out_half.at[xh * 4 + lax.rem(z + 4 - k, 4), rows]
                copies.append(remote(block, block, fwd_s.at[i, k - 1], fwd_r.at[i, k - 1], x_far))
        if order == "z":
            gathers[i][0].wait_recv()
        forwards.append(copies)
        sent += copies
    for copies in forwards:
        for copy in copies:
            copy.wait_recv()
    for copy in sent:
        copy.wait_send()


def fused(grad, first, second, master, old_map, new_map):
    chunks = len(CHUNKS)
    rows = jax.ShapeDtypeStruct((BPD, BLK), f32)
    anywhere = pl.BlockSpec(memory_space=pl.ANY)
    near = pl.BlockSpec(memory_space=pltpu.VMEM)
    sem = pltpu.SemaphoreType.DMA
    return pl.pallas_call(
        kernel,
        out_shape=(rows, rows, rows, jax.ShapeDtypeStruct((8, BPD, BLK), bf16)),
        in_specs=[anywhere] * 6,
        out_specs=(near,) * 4,
        scratch_shapes=[
            pltpu.VMEM((3, BPD, BLK), f32),
            pltpu.VMEM((BPD, BPD), jnp.int32),
            pltpu.VMEM((BPD, BPD), jnp.int32),
            pltpu.VMEM((BPD, BPD), jnp.int32),
            pltpu.VMEM((8, BPD, BLK), bf16),
            pltpu.VMEM((8, BPD, BLK), bf16),
            pltpu.VMEM((8, BPD, BLK), bf16),
            pltpu.VMEM((3, 2, BPD, BLK), bf16),
            pltpu.VMEM((4, BPD, BLK), bf16),
            pltpu.VMEM((3, BPD, BLK), bf16),
            pltpu.VMEM((BPD, BLK), f32),
            pltpu.VMEM((2, 8, 8, 3 * BLK), bf16),
            pltpu.VMEM((2, 8, 8, 3 * BLK), bf16),
            pltpu.VMEM((16, 8, 3 * BLK), bf16),
            pltpu.VMEM((16, 8, 3 * BLK), bf16),
            sem((6,)),
            sem((chunks,)), sem((chunks,)),
            sem((chunks, 7)), sem((chunks, 7)),
            sem((7,)), sem((7,)),
            sem((15,)), sem((15,)),
            sem((chunks, 4)), sem((chunks, 4)),
            sem((chunks, 3)), sem((chunks, 3)),
        ],
        compiler_params=pltpu.CompilerParams(
            collective_id=0, has_side_effects=True, vmem_limit_bytes=48 * 1024 * 1024
        ),
        name="adamw_relayout",
    )(grad, first, second, master, old_map, new_map)


def local(grad_parts, first_moment, second_moment, master, old_map, new_map):
    new_one, new_two, updated, half = fused(
        grad_parts.reshape(8, 2, BPD, BLK),
        first_moment,
        second_moment,
        master,
        old_map.reshape(BPD, BPD),
        new_map.reshape(BPD, BPD),
    )
    return (new_one, new_two, updated, half.reshape(8 * BPD, BLK))


def solution(mesh):
    placed = (
        P("dp", None, "shard", None),
        P(("dp", "shard"), None),
        P(("dp", "shard"), None),
        P(("dp", "shard"), None),
        P(),
        P(),
    )
    return jax.shard_map(
        local,
        mesh=mesh,
        in_specs=placed,
        out_specs=(
            P(("dp", "shard"), None),
            P(("dp", "shard"), None),
            P(("dp", "shard"), None),
            P("dp", None),
        ),
        check_vma=False,
    )
```

time: 162 us -> 66.4 us (0.41)
  waiting for transfers between devices: 117 us -> 0 us
  Pallas kernels: 0 us -> 56.3 us
  between operations: 14.1 us -> 0.65 us
  starting transfers between devices: 11.6 us -> 0 us
  other arithmetic: 7.22 us -> 0 us
  matrix products: 3.3 us -> 0 us
    all_gather x1 -> x0, waiting for transfers between devices: 56.8 us -> none  [local(): lax.all_gather(updated.astype(jnp.bfloat16), 'shard', axis=0, tiled=True)]
    pallas_call x0 -> x1, Pallas kernels: none -> 56.3 us  [fused(): pl.pallas_call(kernel, out_shape=(rows, rows, rows, jax.ShapeDtypeStruct(...]
    all_to_all x1 -> x0, waiting for transfers between devices: 30.2 us -> none  [local(): lax.all_to_all(outgoing, ('dp', 'shard'), split_axis=0, concat_axis=0, ti...]
    reduce_scatter x1 -> x0, waiting for transfers between devices: 29.1 us -> none  [local(): lax.psum_scatter(grad_parts[0].astype(jnp.float32).astype(jnp.bfloat16),...]
    all_to_all x1 -> x0, starting transfers between devices: 11.5 us -> none  [local(): lax.all_to_all(outgoing, ('dp', 'shard'), split_axis=0, concat_axis=0, ti...]
    reduce_or x2 -> x0, other arithmetic: 4.78 us -> none  [owner_table(): found = jnp.any(blocks[:, None, None] == grid[None, :, :], axis=2)]
    unnamed x14, local copies, waits for them, and re-layouts: 4.36 us -> 8.49 us
    dot_general x2 -> x0, matrix products: 3.3 us -> none  [the longest x1 2.35 us: local(): jnp.dot(pick, incoming, precision=lax.Precision.HIGHEST, preferred_elemen...]
  transfers between devices with their start and end apart: 3 -> 0, of which waited for: 3 -> 0; matrix products, arithmetic and copies ran while one was open for 8% -> 0% of each run, Pallas kernels for 0% -> 0%
where the time goes in v1:
time: 66.4 us; the launch traced here: 65.5 us
  Pallas kernels  56.3 us (85%)
  local copies, waits for them, and re-layouts  8.49 us (13%)
    pallas_call x1, Pallas kernels, fused(): pl.pallas_call(kernel, out_shape=(rows, rows, rows, jax.ShapeDtypeStruct(...  56.3 us
    unnamed x14, local copies, waits for them, and re-layouts  8.49 us

profile of v1, /device:TPU:1, one launch (start us, length us, event | category | flops | bytes accessed | tf_op | source)
XLA Modules:
  0.0 65.5 jit_solution(4667095085960136658)
XLA Ops:
  0.6 0.0 copy-start
  0.6 1.0 %copy-done = f32[128,1024]{1,0:T(8,128)S(1)} copy-done((f32[128,1024]{1,0:T(8,128)S(1)}, f32[128,1024]{1,0:T(8,128)}, u32[]{:S(2)}) %copy-start) | copy-done | bytes 524312
  1.7 0.0 copy-start.1
  1.7 1.0 %copy-done.1 = f32[128,1024]{1,0:T(8,128)S(1)} copy-done((f32[128,1024]{1,0:T(8,128)S(1)}, f32[128,1024]{1,0:T(8,128)}, u32[]{:S(2)}) %copy-start.1) | copy-done | bytes 524312
  2.7 0.0 copy-start.2
  2.7 1.0 %copy-done.2 = f32[128,1024]{1,0:T(8,128)S(1)} copy-done((f32[128,1024]{1,0:T(8,128)S(1)}, f32[128,1024]{1,0:T(8,128)}, u32[]{:S(2)}) %copy-start.2) | copy-done | bytes 524312
  3.8 0.0 copy-start.3
  3.8 0.8 %copy-done.3 = s32[16384]{0:T(1024)S(1)} copy-done((s32[16384]{0:T(1024)S(1)}, s32[16384]{0:T(1024)}, u32[]{:S(2)}) %copy-start.3) | copy-done | bytes 65560
  4.6 0.0 copy-start.4
  4.6 0.8 %copy-done.4 = s32[16384]{0:T(1024)S(1)} copy-done((s32[16384]{0:T(1024)S(1)}, s32[16384]{0:T(1024)}, u32[]{:S(2)}) %copy-start.4) | copy-done | bytes 65560
  5.4 56.3 %adamw_relayout.1 = (f32[128,1024]{1,0:T(8,128)S(1)}, f32[128,1024]{1,0:T(8,128)S(1)}, f32[128,1024]{1,0:T(8,128)S(1)}, bf16[8,128,1024]{2,1,0:T(8,128)(2,1)S(1)}) custom-call(bf16[8,2,128,1024]{3,2,1,0:T(8,128)(2,1)} %bitcast.7, f32[128,1024]{1,0:T(8,128)S(1)} %copy-done, f32[128,1024]{1,0:T(8,128)S(1)} %copy-done.1, f32[128,1024]{1,0:T(8,128)S(1)} %copy-done.2, ...), custom_call_target="tpu_custom_call" | custom-call | tf_op jit(solution)/shard_map/adamw_relayout/pallas_call | solution.py:282
  61.8 0.8 %copy.14 = f32[128,1024]{1,0:T(8,128)} copy(f32[128,1024]{1,0:T(8,128)S(1)} %get-tuple-element.16) | data formatting | bytes 1048576
  62.6 0.8 %copy.15 = f32[128,1024]{1,0:T(8,128)} copy(f32[128,1024]{1,0:T(8,128)S(1)} %get-tuple-element.17) | data formatting | bytes 1048576
  63.4 0.8 %copy.16 = f32[128,1024]{1,0:T(8,128)} copy(f32[128,1024]{1,0:T(8,128)S(1)} %get-tuple-element.18) | data formatting | bytes 1048576
  64.2 1.3 %copy.17 = bf16[1024,1024]{1,0:T(8,128)(2,1)} copy(bf16[1024,1024]{1,0:T(8,128)(2,1)S(1)} %bitcast.4) | data formatting | bytes 4194304
Async XLA Ops:
  0.6 1.0 %copy-start = (f32[128,1024]{1,0:T(8,128)S(1)}, f32[128,1024]{1,0:T(8,128)}, u32[]{:S(2)}) copy-start(f32[128,1024]{1,0:T(8,128)} %first.1) | copy-start | bytes 1572868
  1.7 1.0 %copy-start.1 = (f32[128,1024]{1,0:T(8,128)S(1)}, f32[128,1024]{1,0:T(8,128)}, u32[]{:S(2)}) copy-start(f32[128,1024]{1,0:T(8,128)} %second.1) | copy-start | bytes 1572868
  2.7 1.0 %copy-start.2 = (f32[128,1024]{1,0:T(8,128)S(1)}, f32[128,1024]{1,0:T(8,128)}, u32[]{:S(2)}) copy-start(f32[128,1024]{1,0:T(8,128)} %master.1) | copy-start | bytes 1572868
  3.8 0.8 %copy-start.3 = (s32[16384]{0:T(1024)S(1)}, s32[16384]{0:T(1024)}, u32[]{:S(2)}) copy-start(s32[16384]{0:T(1024)} %param.10) | copy-start | bytes 196612
  4.6 0.8 %copy-start.4 = (s32[16384]{0:T(1024)S(1)}, s32[16384]{0:T(1024)}, u32[]{:S(2)}) copy-start(s32[16384]{0:T(1024)} %param.11) | copy-start | bytes 196612

commit v2 on v1

v2 whole, which is shorter than its diff:
```python
import functools

import jax
import jax.numpy as jnp
from jax import lax
from jax.experimental import pallas as pl
from jax.experimental.pallas import tpu as pltpu
from jax.sharding import PartitionSpec as P

beta_one = 0.9
beta_two = 0.95
learning_rate = 0.05
decay_rate = 0.1
epsilon = 1e-08
step_count = 4

MESH = pl.DeviceIdType.MESH
BPD = 128
BLK = 1024
f32 = jnp.float32
bf16 = jnp.bfloat16

CHUNKS = ((0, 16, 'x', 'z'), (16, 16, 'x', 'X'), (32, 16, 'x', 'z'), (48, 16, 'y', 'x'), (64, 32, 'Y', 'z'), (96, 32, 'Y', 'X'))
ORDER = (
    "A0", "P1", "A1", "P2", "P4", "P5", "T0", "R4", "R5", "T1", "pick", "Q4",
    "Q5", "P0", "P3", "S0", "S1", "U4", "Q2", "U5", "Q3", "U2", "Q1", "G4",
    "Q0", "G5", "U1", "U3", "U0", "G2", "G1", "G3", "G0", "H5", "H1",
)
PIECES = ((0, 0, 1024, 0, 0), (1, 0, 512, 0, 1024), (1, 512, 512, 1, 0), (2, 0, 1024, 1, 512))


def adamw(moment_one, moment_two, weights, gradient):
    new_one = beta_one * moment_one + (1.0 - beta_one) * gradient
    new_two = beta_two * moment_two + (1.0 - beta_two) * gradient * gradient
    unbiased_one = new_one / (1.0 - beta_one**step_count)
    unbiased_two = new_two / (1.0 - beta_two**step_count)
    updated = weights - learning_rate * (
        unbiased_one / (jnp.sqrt(unbiased_two) + epsilon) + decay_rate * weights
    )
    return (new_one, new_two, updated)


def owners(wanted_row, table_ref, turned_ref):
    wanted = jnp.broadcast_to(wanted_row, (BPD, BPD)).T
    turned_ref[...] = table_ref[...].T

    def step(k, found):
        return jnp.where(wanted == turned_ref[pl.ds(k, 1), :], 1.0, found)

    return lax.fori_loop(0, BPD, step, jnp.zeros((BPD, BPD), f32), unroll=8)


def swap_matrix():
    row = lax.broadcasted_iota(jnp.int32, (BPD, BPD), 0)
    col = lax.broadcasted_iota(jnp.int32, (BPD, BPD), 1)
    turned = (row & 64) | ((row & 7) << 3) | ((row >> 3) & 7)
    return jnp.where(turned == col, 1.0, 0.0).astype(bf16)


def kernel(
    grad, first, second, master, old_map, new_map,
    out_one, out_two, out_master, out_half,
    states, old_ref, new_ref, turned, own, other, pair, from_y, from_x, part, kept,
    send_a, recv_a, send_b, recv_b,
    load_sem, core_s, core_r, sum_s, sum_r, a_s, a_r, b_s, b_r, gat_s, gat_r, fwd_s, fwd_r,
):
    dp = lax.axis_index("dp")
    sh = lax.axis_index("shard")
    xl, yc = dp // 8, dp % 8
    y, c = yc // 2, yc % 2
    xh, z = sh // 4, sh % 4
    me = dp * 8 + sh

    def at_y(k):
        return (xl * 8 + lax.rem(y + k, 4) * 2 + c, sh)

    def at_z(k):
        return (dp, xh * 4 + lax.rem(z + k, 4))

    x_near = ((1 - xl) * 8 + yc, sh)
    x_far = (dp, (1 - xh) * 4 + z)
    core_mate = (xl * 8 + y * 2 + (1 - c), sh)
    a_places = [lax.rem(yc + k, 8) for k in range(1, 8)]
    a_peers = [(xl * 8 + p, sh) for p in a_places]
    place = xl * 8 + sh
    b_places = [lax.rem(place + k, 16) for k in range(1, 16)]
    b_peers = [((p // 8) * 8 + yc, p % 8) for p in b_places]

    barrier = pltpu.get_barrier_semaphore()
    for peer in a_peers + b_peers:
        pl.semaphore_signal(barrier, inc=1, device_id=peer, device_id_type=MESH)

    loads = [
        pltpu.make_async_copy(new_map, new_ref, load_sem.at[0]),
        pltpu.make_async_copy(old_map, old_ref, load_sem.at[1]),
        pltpu.make_async_copy(first, states.at[0], load_sem.at[2]),
        pltpu.make_async_copy(second, states.at[1], load_sem.at[3]),
        pltpu.make_async_copy(master, states.at[2], load_sem.at[4]),
        pltpu.make_async_copy(grad.at[:, c], own, load_sem.at[5]),
    ]
    for load in loads:
        load.start()
    loads[0].wait()
    loads[1].wait()
    swap = swap_matrix()
    route = owners(old_ref[pl.ds(me, 1), :], new_ref, turned).T.astype(bf16)
    routes = (route, jnp.dot(swap, route, preferred_element_type=f32).astype(bf16))

    pl.semaphore_wait(barrier, 22)

    def remote(src, dst, s_sem, r_sem, peer):
        copy = pltpu.make_async_remote_copy(
            src_ref=src, dst_ref=dst, send_sem=s_sem, recv_sem=r_sem,
            device_id=peer, device_id_type=MESH,
        )
        copy.start()
        return copy

    sent = []

    core = []
    for i, (r0, n, _, _) in enumerate(CHUNKS):
        rows = pl.ds(r0, n)
        core.append(
            remote(grad.at[:, 1 - c, rows], other.at[:, rows], core_s.at[i], core_r.at[i], core_mate)
        )
    sent += core

    def over_a(lane):
        for k in range(7):
            (
                remote(
                    send_a.at[lane, :, a_places[k]], recv_a.at[lane, :, yc],
                    a_s.at[lane], a_r.at[lane], a_peers[k],
                )
            )
        whole = pltpu.make_async_remote_copy(
            src_ref=send_a.at[lane, :, pl.ds(0, 7)], dst_ref=recv_a.at[lane, :, pl.ds(0, 7)],
            send_sem=a_s.at[lane], recv_sem=a_r.at[lane], device_id=a_peers[0], device_id_type=MESH,
        )
        keep = pltpu.make_async_copy(send_a.at[lane, :, yc], recv_a.at[lane, :, yc], load_sem.at[lane])
        keep.start()
        return [whole], keep

    def over_b(lane):
        for k in range(15):
            (
                remote(
                    send_b.at[lane, b_places[k]], recv_b.at[lane, place],
                    b_s.at[lane], b_r.at[lane], b_peers[k],
                )
            )
        whole = pltpu.make_async_remote_copy(
            src_ref=send_b.at[lane, pl.ds(0, 15)], dst_ref=recv_b.at[lane, pl.ds(0, 15)],
            send_sem=b_s.at[lane], recv_sem=b_r.at[lane], device_id=b_peers[0], device_id_type=MESH,
        )
        keep = pltpu.make_async_copy(send_b.at[lane, place], recv_b.at[lane, place], load_sem.at[6 + lane])
        keep.start()
        return [whole], keep

    def arrived(stage):
        for copy in stage[0]:
            copy.wait_recv()
        stage[1].wait()

    def set_out(lane):
        for j, c0, w, of, l0 in PIECES:
            if of == lane:
                if j in pending:
                    pending.pop(j).wait()
                moved = jnp.dot(
                    routes[lane], states[j, :, c0 : c0 + w].astype(bf16), preferred_element_type=f32
                )
                if lane == 0:
                    send_a[0, :, :, :, l0 : l0 + w] = moved.reshape(2, 8, 8, w).astype(bf16)
                else:
                    send_b[1, :, :, l0 : l0 + w] = moved.reshape(16, 8, w).astype(bf16)
        stage_one[lane] = over_a(0) if lane == 0 else over_b(1)
        sent.extend(stage_one[lane][0])

    steps_one, steps_two, gathers, forwards = {}, {}, {}, {}

    def pairs(i):
        r0, n, order, _ = CHUNKS[i]
        rows = pl.ds(r0, n)
        core[i].wait_recv()
        if 3 in pending:
            pending.pop(3).wait()

        def add_pair(q, carry):
            pair[q // 4, q % 4, rows, :] = own[q, rows, :] + other[q, rows, :]
            return carry

        lax.fori_loop(0, 8, add_pair, 0)
        if order == "x":
            copies = [
                remote(pair.at[1 - xl, :, rows], from_x.at[:, rows], sum_s.at[i, 0], sum_r.at[i, 0], x_near)
            ]
        elif order == "d":
            copies = [
                remote(pair.at[1 - xl, y, rows], from_x.at[0, rows], sum_s.at[i, 6], sum_r.at[i, 6], x_near)
            ]
            for k in range(1, 4):
                for side, there in ((0, xl), (1, 1 - xl)):
                    to = lax.rem(y + k, 4)
                    copies.append(
                        remote(
                            pair.at[there, to, rows], from_y.at[k - 1, side, rows],
                            sum_s.at[i, side * 3 + k - 1], sum_r.at[i, side * 3 + k - 1],
                            (there * 8 + to * 2 + c, sh),
                        )
                    )
        elif order == "y":
            copies = []
            for k in range(1, 4):
                copies.append(
                    remote(
                        pair.at[:, lax.rem(y + k, 4), rows], from_y.at[k - 1, :, rows],
                        sum_s.at[i, k - 1], sum_r.at[i, k - 1], at_y(k),
                    )
                )
        else:
            low, high = pl.ds(r0, n // 2), pl.ds(r0 + n // 2, n // 2)
            copies = []
            for k, to, half, slot, peer in (
                (0, 2, low, 1, 1), (1, 2, high, 1, 3), (2, 1, high, 0, 1), (3, 3, low, 2, 3)
            ):
                copies.append(
                    remote(
                        pair.at[:, lax.rem(y + to, 4), half], from_y.at[slot, :, half],
                        sum_s.at[i, k], sum_r.at[i, k], at_y(peer),
                    )
                )
        steps_one[i] = copies
        sent.extend(copies)

    def relay(i):
        r0, n, _, _ = CHUNKS[i]
        for k, to, half in ((0, 1, pl.ds(r0, n // 2)), (1, 3, pl.ds(r0 + n // 2, n // 2))):
            steps_one[i][k].wait_recv()
            place_y = lax.rem(y + to, 4)
            for side in range(2):
                pair[side, place_y, half, :] = pair[side, place_y, half, :] + from_y[1, side, half, :]
            copy = remote(
                pair.at[:, place_y, half], from_y.at[to - 1, :, half],
                sum_s.at[i, 4 + k], sum_r.at[i, 4 + k], at_y(to),
            )
            steps_one[i].append(copy)
            sent.append(copy)
        del steps_one[i][:2]

    def second_axis(i):
        r0, n, order, _ = CHUNKS[i]
        rows = pl.ds(r0, n)
        for copy in steps_one[i]:
            copy.wait_recv()
        copies = []
        if order == "d":
            value = pair[xl, y, rows, :].astype(f32) + from_x[0, rows, :].astype(f32)
            for k in range(3):
                for side in range(2):
                    value = value + from_y[k, side, rows, :].astype(f32)
            kept[rows, :] = value
        elif order == "x":
            for k in range(1, 4):
                to = lax.rem(y + k, 4)
                part[k - 1, rows, :] = pair[xl, to, rows, :] + from_x[to, rows, :]
                copies.append(
                    remote(
                        part.at[k - 1, rows], from_y.at[k - 1, 0, rows],
                        sum_s.at[i, k], sum_r.at[i, k], at_y(k),
                    )
                )
            kept[rows, :] = pair[xl, y, rows, :].astype(f32) + from_x[y, rows, :].astype(f32)
        else:
            def total(side):
                value = pair[side, y, rows, :].astype(f32)
                for k in (0, 1, 2) if order == "y" else (0, 2):
                    value = value + from_y[k, side, rows, :].astype(f32)
                return value

            part[0, rows, :] = total(1 - xl).astype(bf16)
            copies.append(
                remote(part.at[0, rows], from_x.at[0, rows], sum_s.at[i, 6], sum_r.at[i, 6], x_near)
            )
            kept[rows, :] = total(xl)
        steps_two[i] = copies
        sent.extend(copies)

    def update(i):
        r0, n, order, gather = CHUNKS[i]
        rows = pl.ds(r0, n)
        for copy in steps_two[i]:
            copy.wait_recv()
        summed = kept[rows, :]
        if order == "d":
            pass
        elif order == "x":
            for k in range(3):
                summed = summed + from_y[k, 0, rows, :].astype(f32)
        else:
            summed = summed + from_x[0, rows, :].astype(f32)
        new_one, new_two, updated = adamw(
            states[0, rows, :], states[1, rows, :], states[2, rows, :], summed
        )
        out_half[sh, rows, :] = updated.astype(bf16)
        block = out_half.at[sh, rows]
        copies = [remote(block, block, gat_s.at[i, 0], gat_r.at[i, 0], x_far)]
        for k in (1, 2, 3) if gather in "xzd" else (1, 3):
            copies.append(remote(block, block, gat_s.at[i, k], gat_r.at[i, k], at_z(k)))
        if gather == "d":
            for k in range(1, 4):
                far = (dp, (1 - xh) * 4 + lax.rem(z + k, 4))
                copies.append(remote(block, block, fwd_s.at[i, k - 1], fwd_r.at[i, k - 1], far))
        gathers[i] = copies
        sent.extend(copies)
        out_one[rows, :] = new_one
        out_two[rows, :] = new_two
        out_master[rows, :] = updated

    def forward(i):
        r0, n, _, order = CHUNKS[i]
        rows, low, high = pl.ds(r0, n), pl.ds(r0, n // 2), pl.ds(r0 + n // 2, n // 2)
        first_copies = gathers[i]
        copies = []

        def send(block, k, peer):
            copies.append(remote(block, block, fwd_s.at[i, k], fwd_r.at[i, k], peer))

        def behind(k):
            return lax.rem(z + 4 - k, 4)

        if order == "d":
            forwards[i] = first_copies
            return
        if order == "x":
            first_copies[0].wait_recv()
            for k in range(1, 4):
                send(out_half.at[(1 - xh) * 4 + z, rows], k - 1, at_z(k))
            for k in range(1, 4):
                first_copies[k].wait_recv()
        elif order == "z":
            for k in range(1, 4):
                first_copies[k].wait_recv()
                send(out_half.at[xh * 4 + behind(k), rows], k - 1, x_far)
            first_copies[0].wait_recv()
        elif order == "X":
            first_copies[0].wait_recv()
            for k, peer in ((0, 1), (1, 3)):
                send(out_half.at[(1 - xh) * 4 + z, rows], k, at_z(peer))
            for k, peer, half in ((1, 1, low), (2, 3, high)):
                first_copies[k].wait_recv()
                send(out_half.at[xh * 4 + behind(peer), half], k + 1, at_z(peer))
        else:
            for k, peer, half in ((1, 1, low), (2, 3, high)):
                first_copies[k].wait_recv()
                send(out_half.at[xh * 4 + behind(peer), half], k - 1, at_z(peer))
                send(out_half.at[xh * 4 + behind(peer), rows], k + 1, x_far)
            first_copies[0].wait_recv()
        forwards[i] = copies
        sent.extend(copies)

    def hand_on(i):
        r0, n, _, order = CHUNKS[i]
        rows, low, high = pl.ds(r0, n), pl.ds(r0, n // 2), pl.ds(r0 + n // 2, n // 2)
        copies = []
        if order == "X":
            for k, peer, half in ((0, 1, low), (1, 3, high)):
                forwards[i][k].wait_recv()
                block = out_half.at[(1 - xh) * 4 + lax.rem(z + 4 - peer, 4), half]
                copies.append(remote(block, block, fwd_s.at[i, 4 + k], fwd_r.at[i, 4 + k], at_z(peer)))
        else:
            for k in range(2):
                forwards[i][k].wait_recv()
            block = out_half.at[xh * 4 + lax.rem(z + 2, 4), rows]
            copies.append(remote(block, block, fwd_s.at[i, 4], fwd_r.at[i, 4], x_far))
        forwards[i] = forwards[i][2:] + copies
        sent.extend(copies)

    def turn_around(lanes):
        for lane in lanes:
            arrived(stage_one[lane])
            for _, _, w, of, l0 in PIECES:
                if of == lane:
                    source = recv_a[0, :, :, :, l0 : l0 + w] if lane == 0 else recv_b[1, :, :, l0 : l0 + w]
                    came = source.astype(f32).reshape(BPD, w).astype(bf16)
                    moved = jnp.dot(swap, came, preferred_element_type=f32)
                    if lane == 0:
                        send_b[0, :, :, l0 : l0 + w] = moved.reshape(16, 8, w).astype(bf16)
                    else:
                        send_a[1, :, :, :, l0 : l0 + w] = moved.reshape(2, 8, 8, w).astype(bf16)
            stage_two[lane] = over_b(0) if lane == 0 else over_a(1)
            sent.extend(stage_two[lane][0])

    def pick_states(lanes):
        for lane in lanes:
            arrived(stage_two[lane])
            for j, c0, w, of, l0 in PIECES:
                if of == lane:
                    source = recv_b[0, :, :, l0 : l0 + w] if lane == 0 else recv_a[1, :, :, :, l0 : l0 + w]
                    came = source.astype(f32).reshape(BPD, w).astype(bf16)
                    states[j, :, c0 : c0 + w] = jnp.dot(picks[lane], came, preferred_element_type=f32)

    stage_one, stage_two, picks = {}, {}, []
    pending = dict(enumerate(loads[2:6]))
    for step in ORDER:
        if step == "pick":
            pick = owners(new_ref[pl.ds(me, 1), :], old_ref, turned).astype(bf16)
            picks += [jnp.dot(pick, swap, preferred_element_type=f32).astype(bf16), pick]
        elif step[0] == "A":
            set_out(int(step[1]))
        elif step[0] == "T":
            turn_around([int(d) for d in step[1:]])
        elif step[0] == "S":
            pick_states([int(d) for d in step[1:]])
        else:
            act = {"P": pairs, "R": relay, "Q": second_axis, "U": update, "G": forward, "H": hand_on}
            act[step[0]](int(step[1:]))
    last = [copy for copies in forwards.values() for copy in copies]
    for copy in sent:
        if all(copy is not other for other in last):
            copy.wait_send()
    for copy in last:
        copy.wait_recv()
    for copy in last:
        copy.wait_send()


def fused(grad, first, second, master, old_map, new_map):
    chunks = len(CHUNKS)
    rows = jax.ShapeDtypeStruct((BPD, BLK), f32)
    anywhere = pl.BlockSpec(memory_space=pl.ANY)
    near = pl.BlockSpec(memory_space=pltpu.VMEM)
    sem = pltpu.SemaphoreType.DMA
    return pl.pallas_call(
        kernel,
        out_shape=(rows, rows, rows, jax.ShapeDtypeStruct((8, BPD, BLK), bf16)),
        in_specs=[pl.BlockSpec(memory_space=pltpu.HBM)] * 6,
        out_specs=(near,) * 4,
        scratch_shapes=[
            pltpu.VMEM((3, BPD, BLK), f32),
            pltpu.VMEM((BPD, BPD), jnp.int32),
            pltpu.VMEM((BPD, BPD), jnp.int32),
            pltpu.VMEM((BPD, BPD), jnp.int32),
            pltpu.VMEM((8, BPD, BLK), bf16),
            pltpu.VMEM((8, BPD, BLK), bf16),
            pltpu.VMEM((2, 4, BPD, BLK), bf16),
            pltpu.VMEM((3, 2, BPD, BLK), bf16),
            pltpu.VMEM((4, BPD, BLK), bf16),
            pltpu.VMEM((3, BPD, BLK), bf16),
            pltpu.VMEM((BPD, BLK), f32),
            pltpu.VMEM((2, 2, 8, 8, 3 * BLK // 2), bf16),
            pltpu.VMEM((2, 2, 8, 8, 3 * BLK // 2), bf16),
            pltpu.VMEM((2, 16, 8, 3 * BLK // 2), bf16),
            pltpu.VMEM((2, 16, 8, 3 * BLK // 2), bf16),
            sem((8,)),
            sem((chunks,)), sem((chunks,)),
            sem((chunks, 7)), sem((chunks, 7)),
            sem((2,)), sem((2,)),
            sem((2,)), sem((2,)),
            sem((chunks, 4)), sem((chunks, 4)),
            sem((chunks, 6)), sem((chunks, 6)),
        ],
        compiler_params=pltpu.CompilerParams(
            collective_id=0, has_side_effects=True, vmem_limit_bytes=40000 * 1024
        ),
        name="adamw_relayout",
    )(*[pltpu.with_memory_space_constraint(a, pltpu.HBM) for a in (grad, first, second, master, old_map, new_map)])


def settle(*refs):
    sources, targets, sems = refs[:4], refs[4:8], refs[8]
    copies = [
        pltpu.make_async_copy(sources[3].at[pl.ds(4 * i, 4)], targets[3].at[pl.ds(4 * i, 4)], sems.at[i])
        for i in (0, 1)
    ] + [pltpu.make_async_copy(sources[i], targets[i], sems.at[2 + i]) for i in (0, 1, 2)]
    for copy in copies:
        copy.start()
    for copy in copies:
        copy.wait()


def settled(*arrays):
    anywhere = pl.BlockSpec(memory_space=pl.ANY)
    return pl.pallas_call(
        settle,
        out_shape=tuple(jax.ShapeDtypeStruct(a.shape, a.dtype) for a in arrays),
        in_specs=[anywhere] * 4,
        out_specs=(anywhere,) * 4,
        scratch_shapes=[pltpu.SemaphoreType.DMA((5,))],
        compiler_params=pltpu.CompilerParams(vmem_limit_bytes=1024 * 1024),
        name="settle",
    )(*arrays)


def local(grad_parts, first_moment, second_moment, master, old_map, new_map):
    new_one, new_two, updated, half = settled(*fused(
        grad_parts.reshape(8, 2, BPD, BLK),
        first_moment,
        second_moment,
        master,
        old_map.reshape(BPD, BPD),
        new_map.reshape(BPD, BPD),
    ))
    return (new_one, new_two, updated, half.reshape(8 * BPD, BLK))


def solution(mesh):
    placed = (
        P("dp", None, "shard", None),
        P(("dp", "shard"), None),
        P(("dp", "shard"), None),
        P(("dp", "shard"), None),
        P(),
        P(),
    )
    return jax.shard_map(
        local,
        mesh=mesh,
        in_specs=placed,
        out_specs=(
            P(("dp", "shard"), None),
            P(("dp", "shard"), None),
            P(("dp", "shard"), None),
            P("dp", None),
        ),
        check_vma=False,
    )
```

time: 66.4 us -> 52.2 us (0.79); the launches traced: 65.5 us -> 52.1 us
  local copies, waits for them, and re-layouts: 8.49 us -> 0 us
  Pallas kernels: 56.3 us -> 51.5 us
    unnamed x14 -> x0, local copies, waits for them, and re-layouts: 8.49 us -> none
    pallas_call x1, Pallas kernels: 56.3 us -> 49.6 us  [fused(): pl.pallas_call(kernel, out_shape=(rows, rows, rows, jax.ShapeDtypeStruct(...]
    pallas_call x0 -> x1, Pallas kernels: none -> 1.87 us  [settled(): pl.pallas_call(settle, out_shape=tuple((jax.ShapeDtypeStruct(a.shape, a.d...]
where the time goes in v2:
time: 52.2 us; the launch traced here: 52.1 us
  Pallas kernels  51.5 us (99%)
  between operations  0.64 us (1%)
    pallas_call x1, Pallas kernels, fused(): pl.pallas_call(kernel, out_shape=(rows, rows, rows, jax.ShapeDtypeStruct(...  49.6 us
    pallas_call x1, Pallas kernels, settled(): pl.pallas_call(settle, out_shape=tuple((jax.ShapeDtypeStruct(a.shape, a.d...  1.87 us

profile of v2, /device:TPU:1, one launch (start us, length us, event | category | flops | bytes accessed | tf_op | source)
XLA Modules:
  0.0 52.1 jit_solution(4624883083879545720)
XLA Ops:
  0.6 49.6 %adamw_relayout.1 = (f32[128,1024]{1,0:T(8,128)S(1)}, f32[128,1024]{1,0:T(8,128)S(1)}, f32[128,1024]{1,0:T(8,128)S(1)}, bf16[8,128,1024]{2,1,0:T(8,128)(2,1)S(1)}) custom-call(bf16[8,2,128,1024]{3,2,1,0:T(8,128)(2,1)} %bitcast.4, f32[128,1024]{1,0:T(8,128)} %first.1, f32[128,1024]{1,0:T(8,128)} %second.1, f32[128,1024]{1,0:T(8,128)} %master.1, ...), custom_call_target="tpu_custom_call" | custom-call | tf_op jit(solution)/shard_map/adamw_relayout/pallas_call | solution.py:435
  50.2 1.9 %settle.1 = (f32[128,1024]{1,0:T(8,128)}, f32[128,1024]{1,0:T(8,128)}, f32[128,1024]{1,0:T(8,128)}, bf16[8,128,1024]{2,1,0:T(8,128)(2,1)}) custom-call(f32[128,1024]{1,0:T(8,128)S(1)} %get-tuple-element.12.refs_0_, f32[128,1024]{1,0:T(8,128)S(1)} %get-tuple-element.13.refs_1_, f32[128,1024]{1,0:T(8,128)S(1)} %get-tuple-element.14.refs_2_, ...), custom_call_target="tpu_custom_call" | custom-call | tf_op jit(solution)/shard_map/settle/pallas_call | solution.py:485

commit v3 on v2

--- a/solution.py
+++ b/solution.py
@@ -21,6 +21,9 @@
 bf16 = jnp.bfloat16
 
 CHUNKS = ((0, 16, 'x', 'z'), (16, 16, 'x', 'X'), (32, 16, 'x', 'z'), (48, 16, 'y', 'x'), (64, 32, 'Y', 'z'), (96, 32, 'Y', 'X'))
+A_MOVES = ((2, 0), (2, 1), (1, 0), (3, 0), (1, 1), (3, 1), (0, 1))
+B_MOVES = ((2, 2), (1, 2), (3, 2), (2, 1), (2, 3), (1, 1), (3, 3), (1, 3), (3, 1), (2, 0), (0, 2), (1, 0), (0, 1), (3, 0), (0, 3))
+EARLY = (0, 1)
 ORDER = (
     "A0", "P1", "A1", "P2", "P4", "P5", "T0", "R4", "R5", "T1", "pick", "Q4",
     "Q5", "P0", "P3", "S0", "S1", "U4", "Q2", "U5", "Q3", "U2", "Q1", "G4",
@@ -80,11 +83,14 @@
     x_near = ((1 - xl) * 8 + yc, sh)
     x_far = (dp, (1 - xh) * 4 + z)
     core_mate = (xl * 8 + y * 2 + (1 - c), sh)
-    a_places = [lax.rem(yc + k, 8) for k in range(1, 8)]
+    a_places = [lax.rem(y + dy, 4) * 2 + lax.rem(c + dc, 2) for dy, dc in A_MOVES]
     a_peers = [(xl * 8 + p, sh) for p in a_places]
     place = xl * 8 + sh
-    b_places = [lax.rem(place + k, 16) for k in range(1, 16)]
-    b_peers = [((p // 8) * 8 + yc, p % 8) for p in b_places]
+    b_places, b_peers = [], []
+    for dx, dz in B_MOVES:
+        to_x, to_z = lax.rem(xh * 2 + xl + dx, 4), lax.rem(z + dz, 4)
+        b_peers.append((lax.rem(to_x, 2) * 8 + yc, (to_x // 2) * 4 + to_z))
+        b_places.append(lax.rem(to_x, 2) * 8 + (to_x // 2) * 4 + to_z)
 
     barrier = pltpu.get_barrier_semaphore()
     for peer in a_peers + b_peers:
@@ -106,6 +112,22 @@
     route = owners(old_ref[pl.ds(me, 1), :], new_ref, turned).T.astype(bf16)
     routes = (route, jnp.dot(swap, route, preferred_element_type=f32).astype(bf16))
 
+    pending = dict(enumerate(loads[2:6]))
+
+    def set_out(lane):
+        for j, c0, w, of, l0 in PIECES:
+            if of == lane:
+                if j in pending:
+                    pending.pop(j).wait()
+                moved = jnp.dot(
+                    routes[lane], states[j, :, c0 : c0 + w].astype(bf16), preferred_element_type=f32
+                )
+                if lane == 0:
+                    send_a[0, :, :, :, l0 : l0 + w] = moved.reshape(2, 8, 8, w).astype(bf16)
+                else:
+                    send_b[1, :, :, l0 : l0 + w] = moved.reshape(16, 8, w).astype(bf16)
+    for lane in EARLY:
+        set_out(lane)
     pl.semaphore_wait(barrier, 22)
 
     def remote(src, dst, s_sem, r_sem, peer):
@@ -116,15 +138,22 @@
         copy.start()
         return copy
 
+    def joined(src, dst, s_sem, r_sem):
+        return pltpu.make_async_remote_copy(
+            src_ref=src, dst_ref=dst, send_sem=s_sem, recv_sem=r_sem,
+            device_id=core_mate, device_id_type=MESH,
+        )
+
     sent = []
 
-    core = []
-    for i, (r0, n, _, _) in enumerate(CHUNKS):
-        rows = pl.ds(r0, n)
-        core.append(
-            remote(grad.at[:, 1 - c, rows], other.at[:, rows], core_s.at[i], core_r.at[i], core_mate)
+    core = {}
+    for i in [int(step[1:]) for step in ORDER if step[0] == "P"]:
+        rows = pl.ds(*CHUNKS[i][:2])
+        core[i] = remote(
+            grad.at[:, 1 - c, rows], other.at[:, rows], core_s.at[i], core_r.at[i], core_mate
         )
-    sent += core
+        sent.append(core[i])
+
 
     def over_a(lane):
         for k in range(7):
@@ -162,21 +191,6 @@
         for copy in stage[0]:
             copy.wait_recv()
         stage[1].wait()
-
-    def set_out(lane):
-        for j, c0, w, of, l0 in PIECES:
-            if of == lane:
-                if j in pending:
-                    pending.pop(j).wait()
-                moved = jnp.dot(
-                    routes[lane], states[j, :, c0 : c0 + w].astype(bf16), preferred_element_type=f32
-                )
-                if lane == 0:
-                    send_a[0, :, :, :, l0 : l0 + w] = moved.reshape(2, 8, 8, w).astype(bf16)
-                else:
-                    send_b[1, :, :, l0 : l0 + w] = moved.reshape(16, 8, w).astype(bf16)
-        stage_one[lane] = over_a(0) if lane == 0 else over_b(1)
-        sent.extend(stage_one[lane][0])
 
     steps_one, steps_two, gathers, forwards = {}, {}, {}, {}
 
@@ -211,14 +225,14 @@
                         )
                     )
         elif order == "y":
-            copies = []
-            for k in range(1, 4):
-                copies.append(
-                    remote(
-                        pair.at[:, lax.rem(y + k, 4), rows], from_y.at[k - 1, :, rows],
-                        sum_s.at[i, k - 1], sum_r.at[i, k - 1], at_y(k),
-                    )
+            for k in (2, 1, 3):
+                remote(
+                    pair.at[:, lax.rem(y + k, 4), rows], from_y.at[k - 1, :, rows],
+                    sum_s.at[i, 0], sum_r.at[i, 0], at_y(k),
                 )
+            copies = [
+                joined(from_y.at[:, :, rows], from_y.at[:, :, rows], sum_s.at[i, 0], sum_r.at[i, 0])
+            ]
         else:
             low, high = pl.ds(r0, n // 2), pl.ds(r0 + n // 2, n // 2)
             copies = []
@@ -262,15 +276,16 @@
                     value = value + from_y[k, side, rows, :].astype(f32)
             kept[rows, :] = value
         elif order == "x":
-            for k in range(1, 4):
+            for k in (2, 1, 3):
                 to = lax.rem(y + k, 4)
                 part[k - 1, rows, :] = pair[xl, to, rows, :] + from_x[to, rows, :]
-                copies.append(
-                    remote(
-                        part.at[k - 1, rows], from_y.at[k - 1, 0, rows],
-                        sum_s.at[i, k], sum_r.at[i, k], at_y(k),
-                    )
+                remote(
+                    part.at[k - 1, rows], from_y.at[k - 1, 0, rows],
+                    sum_s.at[i, 1], sum_r.at[i, 1], at_y(k),
                 )
+            copies.append(
+                joined(from_y.at[:, 0, rows], from_y.at[:, 0, rows], sum_s.at[i, 1], sum_r.at[i, 1])
+            )
             kept[rows, :] = pair[xl, y, rows, :].astype(f32) + from_x[y, rows, :].astype(f32)
         else:
             def total(side):
@@ -402,13 +417,16 @@
                     states[j, :, c0 : c0 + w] = jnp.dot(picks[lane], came, preferred_element_type=f32)
 
     stage_one, stage_two, picks = {}, {}, []
-    pending = dict(enumerate(loads[2:6]))
     for step in ORDER:
         if step == "pick":
             pick = owners(new_ref[pl.ds(me, 1), :], old_ref, turned).astype(bf16)
             picks += [jnp.dot(pick, swap, preferred_element_type=f32).astype(bf16), pick]
         elif step[0] == "A":
-            set_out(int(step[1]))
+            lane = int(step[1])
+            if lane not in EARLY:
+                set_out(lane)
+            stage_one[lane] = over_a(0) if lane == 0 else over_b(1)
+            sent.extend(stage_one[lane][0])
         elif step[0] == "T":
             turn_around([int(d) for d in step[1:]])
         elif step[0] == "S":

time: 52.2 us -> 51.6 us (0.989)
  Pallas kernels: 51.5 us -> 50.5 us
    pallas_call x1, Pallas kernels: 49.6 us -> 48.6 us  [fused(): pl.pallas_call(kernel, out_shape=(rows, rows, rows, jax.ShapeDtypeStruct(...]
where the time goes in v3:
time: 51.6 us; the launch traced here: 51.1 us
  Pallas kernels  50.5 us (98%)
  between operations  0.64 us (1%)
    pallas_call x1, Pallas kernels, fused(): pl.pallas_call(kernel, out_shape=(rows, rows, rows, jax.ShapeDtypeStruct(...  48.6 us
    pallas_call x1, Pallas kernels, settled(): pl.pallas_call(settle, out_shape=tuple((jax.ShapeDtypeStruct(a.shape, a.d...  1.87 us

profile of v3, /device:TPU:1, one launch (start us, length us, event | category | flops | bytes accessed | tf_op | source)
XLA Modules:
  0.0 51.1 jit_solution(10512534968994234756)
XLA Ops:
  0.6 48.6 %adamw_relayout.1 = (f32[128,1024]{1,0:T(8,128)S(1)}, f32[128,1024]{1,0:T(8,128)S(1)}, f32[128,1024]{1,0:T(8,128)S(1)}, bf16[8,128,1024]{2,1,0:T(8,128)(2,1)S(1)}) custom-call(bf16[8,2,128,1024]{3,2,1,0:T(8,128)(2,1)} %bitcast.4, f32[128,1024]{1,0:T(8,128)} %first.1, f32[128,1024]{1,0:T(8,128)} %second.1, f32[128,1024]{1,0:T(8,128)} %master.1, ...), custom_call_target="tpu_custom_call" | custom-call | tf_op jit(solution)/shard_map/adamw_relayout/pallas_call | solution.py:453
  49.2 1.9 %settle.1 = (f32[128,1024]{1,0:T(8,128)}, f32[128,1024]{1,0:T(8,128)}, f32[128,1024]{1,0:T(8,128)}, bf16[8,128,1024]{2,1,0:T(8,128)(2,1)}) custom-call(f32[128,1024]{1,0:T(8,128)S(1)} %get-tuple-element.12.refs_0_, f32[128,1024]{1,0:T(8,128)S(1)} %get-tuple-element.13.refs_1_, f32[128,1024]{1,0:T(8,128)S(1)} %get-tuple-element.14.refs_2_, ...), custom_call_target="tpu_custom_call" | custom-call | tf_op jit(solution)/shard_map/settle/pallas_call | solution.py:503

commit v4 on v3

--- a/solution.py
+++ b/solution.py
@@ -146,15 +146,6 @@
 
     sent = []
 
-    core = {}
-    for i in [int(step[1:]) for step in ORDER if step[0] == "P"]:
-        rows = pl.ds(*CHUNKS[i][:2])
-        core[i] = remote(
-            grad.at[:, 1 - c, rows], other.at[:, rows], core_s.at[i], core_r.at[i], core_mate
-        )
-        sent.append(core[i])
-
-
     def over_a(lane):
         for k in range(7):
             (
@@ -191,6 +182,20 @@
         for copy in stage[0]:
             copy.wait_recv()
         stage[1].wait()
+
+    stage_one = {}
+    for lane in (0, 1):
+        stage_one[lane] = over_a(0) if lane == 0 else over_b(1)
+        sent.extend(stage_one[lane][0])
+
+    core = {}
+    for i in [int(step[1:]) for step in ORDER if step[0] == "P"]:
+        rows = pl.ds(*CHUNKS[i][:2])
+        core[i] = remote(
+            grad.at[:, 1 - c, rows], other.at[:, rows], core_s.at[i], core_r.at[i], core_mate
+        )
+        sent.append(core[i])
+
 
     steps_one, steps_two, gathers, forwards = {}, {}, {}, {}
 
@@ -416,7 +421,7 @@
                     came = source.astype(f32).reshape(BPD, w).astype(bf16)
                     states[j, :, c0 : c0 + w] = jnp.dot(picks[lane], came, preferred_element_type=f32)
 
-    stage_one, stage_two, picks = {}, {}, []
+    stage_two, picks = {}, []
     for step in ORDER:
         if step == "pick":
             pick = owners(new_ref[pl.ds(me, 1), :], old_ref, turned).astype(bf16)
@@ -425,8 +430,9 @@
             lane = int(step[1])
             if lane not in EARLY:
                 set_out(lane)
-            stage_one[lane] = over_a(0) if lane == 0 else over_b(1)
-            sent.extend(stage_one[lane][0])
+            if lane not in stage_one:
+                stage_one[lane] = over_a(0) if lane == 0 else over_b(1)
+                sent.extend(stage_one[lane][0])
         elif step[0] == "T":
             turn_around([int(d) for d in step[1:]])
         elif step[0] == "S":

time: 51.6 us -> 51.1 us (level)
  no operation moved by 1% of the time
where the time goes in v4:
time: 51.1 us; the launch traced here: 50.7 us
  Pallas kernels  50 us (98%)
  between operations  0.64 us (1%)
    pallas_call x1, Pallas kernels, fused(): pl.pallas_call(kernel, out_shape=(rows, rows, rows, jax.ShapeDtypeStruct(...  48.2 us
    pallas_call x1, Pallas kernels, settled(): pl.pallas_call(settle, out_shape=tuple((jax.ShapeDtypeStruct(a.shape, a.d...  1.87 us

profile of v4, /device:TPU:1, one launch (start us, length us, event | category | flops | bytes accessed | tf_op | source)
XLA Modules:
  0.0 50.7 jit_solution(3853889878743851680)
XLA Ops:
  0.6 48.2 %adamw_relayout.1 = (f32[128,1024]{1,0:T(8,128)S(1)}, f32[128,1024]{1,0:T(8,128)S(1)}, f32[128,1024]{1,0:T(8,128)S(1)}, bf16[8,128,1024]{2,1,0:T(8,128)(2,1)S(1)}) custom-call(bf16[8,2,128,1024]{3,2,1,0:T(8,128)(2,1)} %bitcast.4, f32[128,1024]{1,0:T(8,128)} %first.1, f32[128,1024]{1,0:T(8,128)} %second.1, f32[128,1024]{1,0:T(8,128)} %master.1, ...), custom_call_target="tpu_custom_call" | custom-call | tf_op jit(solution)/shard_map/adamw_relayout/pallas_call | solution.py:459
  48.8 1.9 %settle.1 = (f32[128,1024]{1,0:T(8,128)}, f32[128,1024]{1,0:T(8,128)}, f32[128,1024]{1,0:T(8,128)}, bf16[8,128,1024]{2,1,0:T(8,128)(2,1)}) custom-call(f32[128,1024]{1,0:T(8,128)S(1)} %get-tuple-element.12.refs_0_, f32[128,1024]{1,0:T(8,128)S(1)} %get-tuple-element.13.refs_1_, f32[128,1024]{1,0:T(8,128)S(1)} %get-tuple-element.14.refs_2_, ...), custom_call_target="tpu_custom_call" | custom-call | tf_op jit(solution)/shard_map/settle/pallas_call | solution.py:509
